TPU v7x, 256 devices: a whole 4x4x8 slice. The times are simulated.
256 devices in a mesh: chain: 2 (over core), leaf: 16 (over y, x), head: 8 (over z).
Axes of the slice: x: 4, y: 4, z: 8, core: 2. Of those that a mesh axis runs over, the one named last changes fastest.
Arguments:
- query_in: bfloat16 [16384, 16, 128], P(('chain', 'leaf'), 'head'), may hold values from -6 to 6
- key_in: bfloat16 [16384, 16, 128], P(('chain', 'leaf'), 'head'), may hold values from -120 to 120
- value_in: bfloat16 [16384, 16, 128], P(('chain', 'leaf'), 'head'), may hold values from -6 to 6
- gate_in: bfloat16 [16384, 16, 128], P(('chain', 'leaf'), 'head'), may hold values from -6 to 6
- write_strength: float32 [16, 16384], P('head', ('chain', 'leaf')), as said below
- log_decay: float32 [16, 16384], P('head', ('chain', 'leaf')), as said below
- doc_resets: int32 [256], P(('chain', 'leaf')), may hold values from 0 to 1, as said below
- conv_weight: float32 [3, 4, 16, 128], P(None, None, 'head'), may hold values from -3 to 3
- output_norm_gain: float32 [128], replicated, may hold values from 0.25 to 1.75
- output_projection_weight: bfloat16 [2048, 4096], P(None, 'head'), may hold values from -0.125 to 0.125
Outputs:
- mixed: bfloat16 [16384, 4096], P(('chain', 'leaf'), 'head')
Inputs may be any that keep to these rules, and one draw needn't show every extreme that they name: `write_strength`: strictly positive. `log_decay`: strictly negative. `doc_resets`: at least one block of every draw starts a document.
All inputs are finite; a program needn't handle non-finite values.
Results may differ from a plain program's by a relative error of at most 0.0064.
Values may be sent and summed in bfloat16 or wider, within the bound.
A program may use at most 64 MiB of HBM per device.

v0:
```python
import jax
import jax.numpy as jnp
from jax import lax
from jax.sharding import PartitionSpec as P

BLOCK = 64
highest = lax.Precision.HIGHEST
epsilon = 1e-06
SEQ = ("chain", "leaf")


def mm(spec, a, b):
    return jnp.einsum(spec, a, b, precision=highest, preferred_element_type=jnp.float32)


def from_behind(value, axis, steps):
    count = lax.axis_size(axis)
    initial, last = (max(0, -steps), min(count, count - steps))
    return lax.ppermute(value, axis, [(source, source + steps) for source in range(initial, last)])


def unit_rows(matrix):
    return matrix / jnp.sqrt(jnp.sum(matrix * matrix, axis=-1, keepdims=True) + epsilon)


def causal_filter(signal, rim_rows, weights):
    kernel = weights.shape[0]
    length = signal.shape[0]
    padded = jnp.concatenate([rim_rows, signal], axis=0)
    running = weights[0] * padded[0:length]
    for offset in range(1, kernel):
        running = running + weights[offset] * padded[offset : offset + length]
    return jax.nn.silu(running)


def unit_lower_inverse(lower):
    size = lower.shape[-1]
    row = lax.broadcasted_iota(jnp.int32, (size, size), 0)
    col = lax.broadcasted_iota(jnp.int32, (size, size), 1)
    inverse = jnp.broadcast_to(jnp.eye(size, dtype=jnp.float32), lower.shape)
    span = 1
    while span < size:
        pick = (
            (row // (2 * span) == col // (2 * span))
            & (row // span % 2 == 1)
            & (col // span % 2 == 0)
        )
        coupling = jnp.where(pick, lower, 0.0)
        inverse = lax.optimization_barrier(inverse)
        inverse = inverse - mm(
            "...ij,...jk->...ik", mm("...ij,...jk->...ik", inverse, coupling), inverse
        )
        span *= 2
    return inverse


def on_device(
    query_in,
    key_in,
    value_in,
    gate_in,
    write_strength,
    log_decay,
    doc_resets,
    conv_weight,
    output_norm_gain,
    output_projection_weight,
):
    length, head_count, depth_k = query_in.shape
    value_width = value_in.shape[2]
    kernel = conv_weight.shape[1]
    tail_rows = jnp.stack(
        [
            query_in[length - kernel + 1 :],
            key_in[length - kernel + 1 :],
            value_in[length - kernel + 1 :],
        ]
    )
    rim_rows = from_behind(tail_rows, SEQ, 1)
    query_conv = causal_filter(query_in, rim_rows[0], conv_weight[0])
    key_conv = causal_filter(key_in, rim_rows[1], conv_weight[1])
    value_conv = causal_filter(value_in, rim_rows[2], conv_weight[2])
    query_unit = (unit_rows(query_conv) * depth_k ** (-0.5)).astype(jnp.bfloat16)
    key_unit = unit_rows(key_conv).astype(jnp.bfloat16)
    value_act = value_conv.astype(jnp.bfloat16)
    blocks = length // BLOCK
    query_blk = query_unit.reshape(blocks, BLOCK, head_count, depth_k)
    key_blk = key_unit.reshape(blocks, BLOCK, head_count, depth_k)
    value_blk = value_act.reshape(blocks, BLOCK, head_count, value_width)
    key_gram = jnp.einsum("nthe,nshe->nhts", key_blk, key_blk, preferred_element_type=jnp.float32)
    query_gram = jnp.einsum(
        "nthe,nshe->nhts", query_blk, key_blk, preferred_element_type=jnp.float32
    )
    strength = write_strength.reshape(head_count, blocks, BLOCK).transpose(1, 0, 2)
    decays = log_decay.reshape(head_count, blocks, BLOCK).transpose(1, 0, 2)
    row_index = lax.broadcasted_iota(jnp.int32, (BLOCK, BLOCK), 0)
    col_index = lax.broadcasted_iota(jnp.int32, (BLOCK, BLOCK), 1)
    strict_mask = row_index > col_index
    causal_mask = row_index >= col_index
    cumulative = jnp.cumsum(decays, axis=-1)
    spread_log = cumulative[..., :, None] - cumulative[..., None, :]
    fading = jnp.where(causal_mask, jnp.exp(jnp.where(causal_mask, spread_log, 0.0)), 0.0)
    growth = jnp.exp(cumulative)
    lower = jnp.where(strict_mask, strength[..., :, None] * fading * key_gram, 0.0)
    mixing = fading * query_gram
    query_float = jnp.transpose(query_blk, (0, 2, 1, 3)).astype(jnp.float32)
    key_float = jnp.transpose(key_blk, (0, 2, 1, 3)).astype(jnp.float32)
    value_float = jnp.transpose(value_blk, (0, 2, 1, 3)).astype(jnp.float32)
    targets = jnp.concatenate(
        [strength[..., None] * value_float, (strength * growth)[..., None] * key_float], axis=-1
    )
    solved = mm("nhts,nhsf->nhtf", unit_lower_inverse(lower), targets)
    local_values = solved[..., :value_width]
    write_keys = solved[..., value_width:]
    tail_fade = jnp.exp(cumulative[..., -1:] - cumulative)
    decayed_addresses = tail_fade[..., None] * key_float
    key_eye = jnp.eye(depth_k, dtype=jnp.float32)
    keep_mat = (1 - doc_resets).astype(jnp.float32)[:, None, None, None]
    transition = keep_mat * (
        growth[..., -1, None, None] * key_eye - mm("nhce,nhcf->nhef", decayed_addresses, write_keys)
    )
    addition = mm("nhce,nhcf->nhef", decayed_addresses, local_values)
    query_eff = keep_mat * (
        growth[..., None] * query_float - mm("nhts,nhse->nhte", mixing, write_keys)
    )
    own_output = mm("nhts,nhsf->nhtf", mixing, local_values)
    carry = jnp.concatenate(
        [
            jnp.broadcast_to(key_eye, (head_count, depth_k, depth_k)),
            jnp.zeros((head_count, depth_k, value_width), jnp.float32),
        ],
        axis=-1,
    )
    starts = []
    for n in range(blocks):
        starts.append(carry)
        carry = mm("hij,hjk->hik", transition[n], carry)
        carry = carry.at[..., depth_k:].add(addition[n])
    starts = jnp.stack(starts)
    reach = mm("nhtd,nhde->nhte", query_eff, starts)
    partial_out = own_output + reach[..., depth_k:]
    reach_map = reach[..., :depth_k]
    device_trans = carry[..., :depth_k]
    device_state = carry[..., depth_k:]
    place = lax.axis_index(SEQ)
    count = lax.axis_size(SEQ)
    trans, state = (device_trans, device_state)
    stride = 1
    while stride < count:
        got_trans, got_state = from_behind((trans, state), SEQ, stride)
        has = place >= stride
        state = state + mm("hij,hjk->hik", trans, got_state)
        if stride * 2 < count:
            trans = jnp.where(has, mm("hij,hjk->hik", trans, got_trans), trans)
        stride *= 2
    incoming = from_behind(state, SEQ, 1)
    core = partial_out + mm("nhte,hef->nhtf", reach_map, incoming)
    core = jnp.transpose(core, (0, 2, 1, 3)).reshape(length, head_count, value_width)
    scale_rms = jnp.sqrt(jnp.mean(core * core, axis=-1, keepdims=True) + epsilon)
    normed = (
        core / scale_rms * output_norm_gain * jax.nn.silu(gate_in.astype(jnp.float32))
    ).astype(jnp.bfloat16)
    shard_piece = lax.all_gather(normed, "head", axis=1, tiled=True)
    count = shard_piece.shape[1]
    flat_piece = shard_piece.reshape(shard_piece.shape[0], count * value_width)
    mixed = jnp.dot(flat_piece, output_projection_weight, preferred_element_type=jnp.float32)
    return mixed.astype(jnp.bfloat16)


def solution(mesh):
    return jax.shard_map(
        on_device,
        mesh=mesh,
        in_specs=(
            P(("chain", "leaf"), "head", None),
            P(("chain", "leaf"), "head", None),
            P(("chain", "leaf"), "head", None),
            P(("chain", "leaf"), "head", None),
            P("head", ("chain", "leaf")),
            P("head", ("chain", "leaf")),
            P(("chain", "leaf")),
            P(None, None, "head", None),
            P(),
            P(None, "head"),
        ),
        out_specs=P(("chain", "leaf"), "head"),
        check_vma=False,
    )
```

profile of v0, /device:TPU:2, one launch (start us, length us, event | category | flops | bytes accessed | tf_op | source)
XLA Modules:
  0.0 157.1 jit_solution(13814795067078425158)
XLA Ops:
  6.5 1.1 copy.162
  7.7 1.0 copy.161
  8.7 1.0 copy.160
  10.3 3.4 %collective-permute-start = (bf16[3,3,2,128]{3,1,2,0:T(4,128)(2,1)}, bf16[3,3,2,128]{3,1,2,0:T(4,128)(2,1)}, u32[]{:S(2)}, u32[]{:S(2)}) collective-permute-start(bf16[3,3,2,128]{3,1,2,0:T(4,128)(2,1)} %pad_maximum_fusion.3), channel_id=1, source_target_pairs={{0,8},{8,16},{16,24},{24,32},{32,40},{40,48},{48,56},{56,64},{64,7... | collective-permute-start | bytes 13832 | tf_op jit(solution)/shard_map/ppermute | solution.py:19
  14.5 1.5 slice_bitcast_fusion.33
  15.9 0.8 reshape.339
  16.7 0.8 reshape.342
  18.1 1.1 subtract_convert_fusion
  19.2 0.7 fusion.41
  20.6 0.8 fusion.122
  23.9 0.8 broadcast_in_dim.62
  27.5 1.4 multiply_reduce_fusion.1
  38.0 1.0 fusion.5
  39.0 2.2 %fusion.15 = f32[8,2,128,128]{3,2,1,0:T(8,128)S(1)} fusion(f32[8,2,64,256]{3,2,1,0:T(8,128)S(1)} %fusion.5, f32[8,2,64]{2,1,0:T(2,128)S(1)} %copy.181, bf16[8,64,2,128]{3,1,0,2:T(8,128)(2,1)S(1)} %bitcast.218), kind=kOutput, calls=%fused_computation.43 | convolution fusion | flops 201588736 | bytes 1843200 | tf_op jit(solution)/shard_map/nhce,nhcf->nhef/dot_general | solution.py:13
  41.3 2.0 %fusion = f32[8,2,128,128]{3,2,1,0:T(8,128)S(1)} fusion(f32[128,128]{1,0:T(8,128)S(1)} %copy-done.3, f32[8,2]{1,0:T(8,128)S(1)} %bitcast.226, f32[8]{0:T(128)S(1)} %copy-done.21, f32[8,2,64,256]{3,2,1,0:T(8,128)S(1)} %fusion.5, f32[8,2,64]{2,1,0:T(2,128)S(1)} %copy.181, bf16[8,64,2,128]{3,1,0,2:T(8,128)(2,1)S(1)} %bitcast.219), kind=kOutput, calls=%fused_computation.1 | convolution fusion | flops 202375168 | bytes 1913344 | tf_op jit(solution)/shard_map/nhce,nhcf->nhef/dot_general | solution.py:13
  46.6 3.1 %collective-permute-start.2 = (f32[2,128,128]{2,1,0:T(8,128)S(1)}, f32[2,128,128]{2,1,0:T(8,128)S(1)}, u32[]{:S(2)}, u32[]{:S(2)}) collective-permute-start(f32[2,128,128]{2,1,0:T(8,128)S(1)} %get-tuple-element.105), channel_id=1, source_target_pairs={{0,8},{8,16},{16,24},{24,32},{32,40},{40,48},{48,56},{56,64},{64,7... | collective-permute-start | bytes 393224 | tf_op jit(solution)/shard_map/ppermute | solution.py:19
  49.7 3.4 %collective-permute-start.1 = (f32[2,128,128]{2,1,0:T(8,128)S(1)}, f32[2,128,128]{2,1,0:T(8,128)S(1)}, u32[]{:S(2)}, u32[]{:S(2)}) collective-permute-start(f32[2,128,128]{2,1,0:T(8,128)S(1)} %get-tuple-element.106), channel_id=1, source_target_pairs={{0,8},{8,16},{16,24},{24,32},{32,40},{40,48},{48,56},{56,64},{64,7... | collective-permute-start | bytes 393224 | tf_op jit(solution)/shard_map/ppermute | solution.py:19
  55.0 1.3 fusion.140
  56.8 4.3 %collective-permute-start.3 = (f32[2,128,128]{2,1,0:T(8,128)S(1)}, f32[2,128,128]{2,1,0:T(8,128)S(1)}, u32[]{:S(2)}, u32[]{:S(2)}) collective-permute-start(f32[2,128,128]{2,1,0:T(8,128)S(1)} %convolution_add_fusion.5), channel_id=1, source_target_pairs={{0,16},{8,24},{16,32},{24,40},{32,48},{40,56},{48,64},{56,72},{64,... | collective-permute-start | bytes 393224 | tf_op jit(solution)/shard_map/ppermute | solution.py:19
  61.4 4.0 %collective-permute-start.4 = (f32[2,128,128]{2,1,0:T(8,128)S(1)}, f32[2,128,128]{2,1,0:T(8,128)S(1)}, u32[]{:S(2)}, u32[]{:S(2)}) collective-permute-start(f32[2,128,128]{2,1,0:T(8,128)S(1)} %convolution_select_fusion.3), channel_id=1, source_target_pairs={{0,16},{8,24},{16,32},{24,40},{32,48},{40,56},{48,64},{56,72},{64,... | collective-permute-start | bytes 393224 | tf_op jit(solution)/shard_map/ppermute | solution.py:19
  65.7 4.1 %collective-permute-start.5 = (f32[2,128,128]{2,1,0:T(8,128)S(1)}, f32[2,128,128]{2,1,0:T(8,128)S(1)}, u32[]{:S(2)}, u32[]{:S(2)}) collective-permute-start(f32[2,128,128]{2,1,0:T(8,128)S(1)} %convolution_add_fusion.4), channel_id=1, source_target_pairs={{0,32},{8,40},{16,48},{24,56},{32,64},{40,72},{48,80},{56,88},{64,... | collective-permute-start | bytes 393224 | tf_op jit(solution)/shard_map/ppermute | solution.py:19
  70.1 4.4 %collective-permute-start.6 = (f32[2,128,128]{2,1,0:T(8,128)S(1)}, f32[2,128,128]{2,1,0:T(8,128)S(1)}, u32[]{:S(2)}, u32[]{:S(2)}) collective-permute-start(f32[2,128,128]{2,1,0:T(8,128)S(1)} %convolution_select_fusion.2), channel_id=1, source_target_pairs={{0,32},{8,40},{16,48},{24,56},{32,64},{40,72},{48,80},{56,88},{64,... | collective-permute-start | bytes 393224 | tf_op jit(solution)/shard_map/ppermute | solution.py:19
  74.8 4.5 %collective-permute-start.7 = (f32[2,128,128]{2,1,0:T(8,128)S(1)}, f32[2,128,128]{2,1,0:T(8,128)S(1)}, u32[]{:S(2)}, u32[]{:S(2)}) collective-permute-start(f32[2,128,128]{2,1,0:T(8,128)S(1)} %convolution_add_fusion.3), channel_id=1, source_target_pairs={{0,64},{8,72},{16,80},{24,88},{32,96},{40,104},{48,112},{56,120},{... | collective-permute-start | bytes 393224 | tf_op jit(solution)/shard_map/ppermute | solution.py:19
  79.6 3.4 %collective-permute-start.8 = (f32[2,128,128]{2,1,0:T(8,128)S(1)}, f32[2,128,128]{2,1,0:T(8,128)S(1)}, u32[]{:S(2)}, u32[]{:S(2)}) collective-permute-start(f32[2,128,128]{2,1,0:T(8,128)S(1)} %convolution_select_fusion.1), channel_id=1, source_target_pairs={{0,64},{8,72},{16,80},{24,88},{32,96},{40,104},{48,112},{56,120},{... | collective-permute-start | bytes 393224 | tf_op jit(solution)/shard_map/ppermute | solution.py:19
  83.3 1.8 %collective-permute-start.9 = (f32[2,128,128]{2,1,0:T(8,128)S(1)}, f32[2,128,128]{2,1,0:T(8,128)S(1)}, u32[]{:S(2)}, u32[]{:S(2)}) collective-permute-start(f32[2,128,128]{2,1,0:T(8,128)S(1)} %convolution_add_fusion.2), channel_id=1, source_target_pairs={{0,128},{8,136},{16,144},{24,152},{32,160},{40,168},{48,176},{56,1... | collective-permute-start | bytes 393224 | tf_op jit(solution)/shard_map/ppermute | solution.py:19
  86.4 5.1 %collective-permute-start.10 = (f32[2,128,128]{2,1,0:T(8,128)S(1)}, f32[2,128,128]{2,1,0:T(8,128)S(1)}, u32[]{:S(2)}, u32[]{:S(2)}) collective-permute-start(f32[2,128,128]{2,1,0:T(8,128)S(1)} %convolution_add_fusion.1), channel_id=1, source_target_pairs={{0,8},{8,16},{16,24},{24,32},{32,40},{40,48},{48,56},{56,64},{64,7... | collective-permute-start | bytes 393224 | tf_op jit(solution)/shard_map/ppermute | solution.py:19
  92.2 3.1 %collective-permute-done.10 = f32[2,128,128]{2,1,0:T(8,128)S(1)} collective-permute-done((f32[2,128,128]{2,1,0:T(8,128)S(1)}, f32[2,128,128]{2,1,0:T(8,128)S(1)}, u32[]{:S(2)}, u32[]{:S(2)}) %collective-permute-start.10) | collective-permute-done | bytes 131104 | tf_op jit(solution)/shard_map/ppermute | solution.py:19
  95.2 0.8 multiply_reduce_fusion
  96.1 0.9 fusion.28
  97.1 45.5 %all-gather.2.cloned.1.call-done = bf16[512,16,128]{2,0,1:T(8,128)(2,1)} async-done(((bf16[512,2,128]{2,0,1:T(8,128)(2,1)}), bf16[512,16,128]{2,0,1:T(8,128)(2,1)}) %all-gather.2.cloned.1.call-update) | async-done | bytes 2097168 | tf_op jit(solution)/shard_map/all_gather | solution.py:163
  142.7 3.9 %copy.185 = bf16[512,16,128]{0,2,1:T(8,128)(2,1)} copy(bf16[512,16,128]{2,0,1:T(8,128)(2,1)} %all-gather.2.cloned.1.call-done) | data formatting | bytes 4194304 | tf_op jit(solution)/shard_map/all_gather | solution.py:163
  146.6 3.7 %convolution_convert_fusion = bf16[512,512]{1,0:T(8,128)(2,1)} fusion(bf16[512,2048]{0,1:T(8,128)(2,1)} %bitcast.215, bf16[2048,512]{1,0:T(8,128)(2,1)S(1)} %copy-done), kind=kOutput, calls=%fused_computation.2 | convolution fusion | flops 1074003968 | bytes 4718592 | tf_op jit(solution)/shard_map/dot_general | solution.py:166
  (144 shorter events, 25.6 us)
Async XLA Ops:
  6.5 140.1 %copy-start = (bf16[2048,512]{1,0:T(8,128)(2,1)S(1)}, bf16[2048,512]{1,0:T(8,128)(2,1)}, u32[]{:S(2)}) copy-start(bf16[2048,512]{1,0:T(8,128)(2,1)} %param.35) | copy-start | bytes 6291460
  6.5 136.1 %all-gather.2.cloned.1.call-start = ((), (), s32[]{:S(2)}) async-start(), calls=%async_computation | async-start | bytes 2359296 | tf_op jit(solution)/shard_map/all_gather | solution.py:163
  10.3 16.5 %collective-permute-start = (bf16[3,3,2,128]{3,1,2,0:T(4,128)(2,1)}, bf16[3,3,2,128]{3,1,2,0:T(4,128)(2,1)}, u32[]{:S(2)}, u32[]{:S(2)}) collective-permute-start(bf16[3,3,2,128]{3,1,2,0:T(4,128)(2,1)} %pad_maximum_fusion.3), channel_id=1, source_target_pairs={{0,8},{8,16},{16,24},{24,32},{32,40},{40,48},{48,56},{56,64},{64,7... | collective-permute-start | bytes 13832 | tf_op jit(solution)/shard_map/ppermute | solution.py:19
  14.4 8.9 %copy-start.2 = (f32[128,128]{1,0:T(8,128)}, f32[128,128]{1,0:T(8,128)S(1)}, u32[]{:S(2)}) copy-start(f32[128,128]{1,0:T(8,128)S(1)} %fusion.84) | copy-start | bytes 196612
  26.8 2.4 %copy-start.11 = (f32[8,2,64]{2,1,0:T(2,128)S(1)}, f32[8,2,64]{2,1,0:T(2,128)}, u32[]{:S(2)}) copy-start(f32[8,2,64]{2,1,0:T(2,128)} %copy.169) | copy-start | bytes 12292
  26.8 2.4 %copy-start.14 = (pred[64,64]{1,0:T(8,128)(4,1)S(1)}, pred[64,64]{1,0:T(8,128)(4,1)}, u32[]{:S(2)}) copy-start(pred[64,64]{1,0:T(8,128)(4,1)} %get-tuple-element.135) | copy-start | bytes 12292
  26.8 2.4 %copy-start.15 = (f32[8,2,64]{2,1,0:T(2,128)S(1)}, f32[8,2,64]{2,1,0:T(2,128)}, u32[]{:S(2)}) copy-start(f32[8,2,64]{2,1,0:T(2,128)} %copy.158) | copy-start | bytes 12292
  26.8 2.4 %copy-start.16 = (pred[64,64]{1,0:T(8,128)(4,1)S(1)}, pred[64,64]{1,0:T(8,128)(4,1)}, u32[]{:S(2)}) copy-start(pred[64,64]{1,0:T(8,128)(4,1)} %get-tuple-element.134) | copy-start | bytes 12292
  26.8 2.8 %copy-start.9 = (pred[64,64]{1,0:T(8,128)(4,1)S(1)}, pred[64,64]{1,0:T(8,128)(4,1)}, u32[]{:S(2)}) copy-start(pred[64,64]{1,0:T(8,128)(4,1)} %get-tuple-element.130) | copy-start | bytes 12292
  30.3 2.0 %copy-start.7 = (pred[64,64]{1,0:T(8,128)(4,1)S(1)}, pred[64,64]{1,0:T(8,128)(4,1)}, u32[]{:S(2)}) copy-start(pred[64,64]{1,0:T(8,128)(4,1)} %get-tuple-element.128) | copy-start | bytes 12292
  31.6 2.0 %copy-start.6 = (pred[64,64]{1,0:T(8,128)(4,1)S(1)}, pred[64,64]{1,0:T(8,128)(4,1)}, u32[]{:S(2)}) copy-start(pred[64,64]{1,0:T(8,128)(4,1)} %get-tuple-element.127) | copy-start | bytes 12292
  32.9 2.0 %copy-start.5 = (pred[64,64]{1,0:T(8,128)(4,1)S(1)}, pred[64,64]{1,0:T(8,128)(4,1)}, u32[]{:S(2)}) copy-start(pred[64,64]{1,0:T(8,128)(4,1)} %get-tuple-element.126) | copy-start | bytes 12292
  38.0 3.2 %copy-start.3 = (f32[128,128]{1,0:T(8,128)S(1)}, f32[128,128]{1,0:T(8,128)}, u32[]{:S(2)}) copy-start(f32[128,128]{1,0:T(8,128)} %copy-done.2) | copy-start | bytes 196612
  38.0 3.2 %copy-start.13 = (f32[8,2,1]{1,0,2:T(8,128)S(1)}, f32[8,2,1]{1,0,2:T(8,128)}, u32[]{:S(2)}) copy-start(f32[8,2,1]{1,0,2:T(8,128)} %copy.186) | copy-start | bytes 196
  38.0 3.2 %copy-start.21 = (f32[8]{0:T(128)S(1)}, f32[8]{0:T(128)}, u32[]{:S(2)}) copy-start(f32[8]{0:T(128)} %subtract_convert_fusion) | copy-start | bytes 100
  44.9 8.2 %copy-start.1 = (f32[8,2,128,256]{3,2,1,0:T(8,128)S(1)}, f32[8,2,128,256]{3,2,1,0:T(8,128)}, u32[]{:S(2)}) copy-start(f32[8,2,128,256]{3,2,1,0:T(8,128)} %fusion.41) | copy-start | bytes 6291460
  46.5 6.8 %copy-start.17 = (f32[2,128]{1,0:T(2,128)S(1)}, f32[2,128]{1,0:T(2,128)}, u32[]{:S(2)}) copy-start(f32[2,128]{1,0:T(2,128)} %get-tuple-element.113) | copy-start | bytes 3076
  46.5 6.8 %copy-start.18 = (f32[2,128]{1,0:T(2,128)S(1)}, f32[2,128]{1,0:T(2,128)}, u32[]{:S(2)}) copy-start(f32[2,128]{1,0:T(2,128)} %get-tuple-element.114) | copy-start | bytes 3076
  46.5 6.8 %copy-start.19 = (f32[2,128]{1,0:T(2,128)S(1)}, f32[2,128]{1,0:T(2,128)}, u32[]{:S(2)}) copy-start(f32[2,128]{1,0:T(2,128)} %get-tuple-element.115) | copy-start | bytes 3076
  46.5 6.8 %copy-start.20 = (f32[2,128]{1,0:T(2,128)S(1)}, f32[2,128]{1,0:T(2,128)}, u32[]{:S(2)}) copy-start(f32[2,128]{1,0:T(2,128)} %get-tuple-element.116) | copy-start | bytes 3076
  46.6 14.6 %collective-permute-start.2 = (f32[2,128,128]{2,1,0:T(8,128)S(1)}, f32[2,128,128]{2,1,0:T(8,128)S(1)}, u32[]{:S(2)}, u32[]{:S(2)}) collective-permute-start(f32[2,128,128]{2,1,0:T(8,128)S(1)} %get-tuple-element.105), channel_id=1, source_target_pairs={{0,8},{8,16},{16,24},{24,32},{32,40},{40,48},{48,56},{56,64},{64,7... | collective-permute-start | bytes 393224 | tf_op jit(solution)/shard_map/ppermute | solution.py:19
  49.7 6.9 %collective-permute-start.1 = (f32[2,128,128]{2,1,0:T(8,128)S(1)}, f32[2,128,128]{2,1,0:T(8,128)S(1)}, u32[]{:S(2)}, u32[]{:S(2)}) collective-permute-start(f32[2,128,128]{2,1,0:T(8,128)S(1)} %get-tuple-element.106), channel_id=1, source_target_pairs={{0,8},{8,16},{16,24},{24,32},{32,40},{40,48},{48,56},{56,64},{64,7... | collective-permute-start | bytes 393224 | tf_op jit(solution)/shard_map/ppermute | solution.py:19
  56.8 8.7 %collective-permute-start.3 = (f32[2,128,128]{2,1,0:T(8,128)S(1)}, f32[2,128,128]{2,1,0:T(8,128)S(1)}, u32[]{:S(2)}, u32[]{:S(2)}) collective-permute-start(f32[2,128,128]{2,1,0:T(8,128)S(1)} %convolution_add_fusion.5), channel_id=1, source_target_pairs={{0,16},{8,24},{16,32},{24,40},{32,48},{40,56},{48,64},{56,72},{64,... | collective-permute-start | bytes 393224 | tf_op jit(solution)/shard_map/ppermute | solution.py:19
  61.4 8.4 %collective-permute-start.4 = (f32[2,128,128]{2,1,0:T(8,128)S(1)}, f32[2,128,128]{2,1,0:T(8,128)S(1)}, u32[]{:S(2)}, u32[]{:S(2)}) collective-permute-start(f32[2,128,128]{2,1,0:T(8,128)S(1)} %convolution_select_fusion.3), channel_id=1, source_target_pairs={{0,16},{8,24},{16,32},{24,40},{32,48},{40,56},{48,64},{56,72},{64,... | collective-permute-start | bytes 393224 | tf_op jit(solution)/shard_map/ppermute | solution.py:19
  65.7 8.8 %collective-permute-start.5 = (f32[2,128,128]{2,1,0:T(8,128)S(1)}, f32[2,128,128]{2,1,0:T(8,128)S(1)}, u32[]{:S(2)}, u32[]{:S(2)}) collective-permute-start(f32[2,128,128]{2,1,0:T(8,128)S(1)} %convolution_add_fusion.4), channel_id=1, source_target_pairs={{0,32},{8,40},{16,48},{24,56},{32,64},{40,72},{48,80},{56,88},{64,... | collective-permute-start | bytes 393224 | tf_op jit(solution)/shard_map/ppermute | solution.py:19
  70.1 9.2 %collective-permute-start.6 = (f32[2,128,128]{2,1,0:T(8,128)S(1)}, f32[2,128,128]{2,1,0:T(8,128)S(1)}, u32[]{:S(2)}, u32[]{:S(2)}) collective-permute-start(f32[2,128,128]{2,1,0:T(8,128)S(1)} %convolution_select_fusion.2), channel_id=1, source_target_pairs={{0,32},{8,40},{16,48},{24,56},{32,64},{40,72},{48,80},{56,88},{64,... | collective-permute-start | bytes 393224 | tf_op jit(solution)/shard_map/ppermute | solution.py:19
  74.8 8.2 %collective-permute-start.7 = (f32[2,128,128]{2,1,0:T(8,128)S(1)}, f32[2,128,128]{2,1,0:T(8,128)S(1)}, u32[]{:S(2)}, u32[]{:S(2)}) collective-permute-start(f32[2,128,128]{2,1,0:T(8,128)S(1)} %convolution_add_fusion.3), channel_id=1, source_target_pairs={{0,64},{8,72},{16,80},{24,88},{32,96},{40,104},{48,112},{56,120},{... | collective-permute-start | bytes 393224 | tf_op jit(solution)/shard_map/ppermute | solution.py:19
  79.6 5.9 %collective-permute-start.8 = (f32[2,128,128]{2,1,0:T(8,128)S(1)}, f32[2,128,128]{2,1,0:T(8,128)S(1)}, u32[]{:S(2)}, u32[]{:S(2)}) collective-permute-start(f32[2,128,128]{2,1,0:T(8,128)S(1)} %convolution_select_fusion.1), channel_id=1, source_target_pairs={{0,64},{8,72},{16,80},{24,88},{32,96},{40,104},{48,112},{56,120},{... | collective-permute-start | bytes 393224 | tf_op jit(solution)/shard_map/ppermute | solution.py:19
  83.3 2.8 %collective-permute-start.9 = (f32[2,128,128]{2,1,0:T(8,128)S(1)}, f32[2,128,128]{2,1,0:T(8,128)S(1)}, u32[]{:S(2)}, u32[]{:S(2)}) collective-permute-start(f32[2,128,128]{2,1,0:T(8,128)S(1)} %convolution_add_fusion.2), channel_id=1, source_target_pairs={{0,128},{8,136},{16,144},{24,152},{32,160},{40,168},{48,176},{56,1... | collective-permute-start | bytes 393224 | tf_op jit(solution)/shard_map/ppermute | solution.py:19
  86.4 9.8 %copy-start.4 = (bf16[512,2,128]{2,1,0:T(2,128)(2,1)S(1)}, bf16[512,2,128]{2,1,0:T(2,128)(2,1)}, u32[]{:S(2)}) copy-start(bf16[512,2,128]{2,1,0:T(2,128)(2,1)} %param.29) | copy-start | bytes 786436
  86.4 9.8 %copy-start.22 = (f32[128]{0:T(128)S(1)}, f32[128]{0:T(128)}, u32[]{:S(2)}) copy-start(f32[128]{0:T(128)} %param.34) | copy-start | bytes 1540
  86.4 8.8 %collective-permute-start.10 = (f32[2,128,128]{2,1,0:T(8,128)S(1)}, f32[2,128,128]{2,1,0:T(8,128)S(1)}, u32[]{:S(2)}, u32[]{:S(2)}) collective-permute-start(f32[2,128,128]{2,1,0:T(8,128)S(1)} %convolution_add_fusion.1), channel_id=1, source_target_pairs={{0,8},{8,16},{16,24},{24,32},{32,40},{40,48},{48,56},{56,64},{64,7... | collective-permute-start | bytes 393224 | tf_op jit(solution)/shard_map/ppermute | solution.py:19
  (3 other events, 4.8 us)
Sparse Core Ops, SparseCore 0:
  97.2 45.3 all-gather.1
where the time goes:
time: 158 us; the launch traced here: 157 us
  waiting for transfers between devices  49.5 us (31%)
  starting transfers between devices  41.6 us (26%)
  matrix products  26 us (16%)
  local copies, waits for them, and re-layouts  16.7 us (11%)
  between operations  14.4 us (9%)
  other arithmetic  8.9 us (6%)
    all_gather x1, waiting for transfers between devices, on_device(): shard_piece = lax.all_gather(normed, 'head', axis=1, tiled=True)  45.5 us
    ppermute x11, starting transfers between devices, from_behind(): lax.ppermute(value, axis, [(source, source + steps) for source in range(i...  41.6 us
    dot_general x36, matrix products, mm(): jnp.einsum(spec, a, b, precision=highest, preferred_element_type=jnp.floa...  21.7 us
    unnamed x56, local copies, waits for them, and re-layouts  4.06 us
    ppermute x11, waiting for transfers between devices, from_behind(): lax.ppermute(value, axis, [(source, source + steps) for source in range(i...  3.97 us
    all_gather x1, local copies, waits for them, and re-layouts, on_device(): shard_piece = lax.all_gather(normed, 'head', axis=1, tiled=True)  3.93 us
    dot_general x1, matrix products, on_device(): jnp.dot(flat_piece, output_projection_weight, preferred_element_type=jnp....  3.65 us
  transfers between devices with their start and end apart: 12, of which 5 were waited for; matrix products, arithmetic and copies ran while one was open for 12% of the time, Pallas kernels for 0%

commit v1 on v0

--- a/solution.py
+++ b/solution.py
@@ -1,3 +1,4 @@
+import functools
 import jax
 import jax.numpy as jnp
 from jax import lax
@@ -7,6 +8,38 @@
 highest = lax.Precision.HIGHEST
 epsilon = 1e-06
 SEQ = ("chain", "leaf")
+
+
+def set_domain_now(panel, array_dim):
+    panel = jnp.moveaxis(panel, 0, array_dim)
+    f_now = panel.shape
+    return panel.reshape(
+        *f_now[:array_dim], f_now[array_dim] * f_now[array_dim + 1], *f_now[array_dim + 2 :]
+    )
+
+
+def enter_targets(z_in, bus_axis, join_dim):
+    k_all = lax.axis_size(bus_axis)
+    buffers = tuple(((q, (q + 1) % k_all) for q in range(k_all)))
+    inbox = tuple(((src_i, i0) for i0, src_i in buffers))
+    s_next, block_out = ([], [])
+    for it in range(k_all - 1):
+        if it % 2 == 0:
+            high = lax.ppermute(s_next[-1] if s_next else z_in, axis_name=bus_axis, perm=buffers)
+            s_next.append(high)
+        else:
+            block_out.append(
+                lax.ppermute(block_out[-1] if block_out else z_in, axis_name=bus_axis, perm=inbox)
+            )
+    arr_out = jnp.stack([*s_next[::-1], z_in, *block_out], 0)
+    b_next = len(s_next)
+    heard = lax.axis_index(bus_axis)
+    low = heard - b_next
+    arr_out = arr_out[(jnp.arange(k_all) - low) % k_all]
+    return set_domain_now(arr_out, join_dim)
+
+
+choose_the_pieces_all = functools.partial(enter_targets, bus_axis="head", join_dim=1)
 
 
 def mm(spec, a, b):
@@ -160,7 +193,7 @@
     normed = (
         core / scale_rms * output_norm_gain * jax.nn.silu(gate_in.astype(jnp.float32))
     ).astype(jnp.bfloat16)
-    shard_piece = lax.all_gather(normed, "head", axis=1, tiled=True)
+    shard_piece = choose_the_pieces_all(normed)
     count = shard_piece.shape[1]
     flat_piece = shard_piece.reshape(shard_piece.shape[0], count * value_width)
     mixed = jnp.dot(flat_piece, output_projection_weight, preferred_element_type=jnp.float32)

time: 158 us -> 152 us (0.962); the launches traced: 157 us -> 149 us
  waiting for transfers between devices: 49.5 us -> 29.8 us
  between operations: 14.4 us -> 1.07 us
  local copies, waits for them, and re-layouts: 16.7 us -> 28.5 us
  starting transfers between devices: 41.6 us -> 53.4 us
    all_gather x1 -> x0, waiting for transfers between devices: 45.5 us -> none  [on_device(): shard_piece = lax.all_gather(normed, 'head', axis=1, tiled=True)]
    ppermute x0 -> x7, waiting for transfers between devices: none -> 25.9 us  [the longest x4 25.8 us: enter_targets(): lax.ppermute(s_next[-1] if s_next else z_in, axis_name=bus_axis, perm=buf...]
    ppermute x0 -> x7, starting transfers between devices: none -> 11.8 us  [the longest x3 9.78 us: enter_targets(): lax.ppermute(block_out[-1] if block_out else z_in, axis_name=bus_axis, pe...]
    unnamed x56 -> x69, local copies, waits for them, and re-layouts: 4.06 us -> 11.3 us
    all_gather x1 -> x0, local copies, waits for them, and re-layouts: 3.93 us -> none  [on_device(): shard_piece = lax.all_gather(normed, 'head', axis=1, tiled=True)]
    transpose x0 -> x1, local copies, waits for them, and re-layouts: none -> 3.92 us  [set_domain_now(): panel = jnp.moveaxis(panel, 0, array_dim)]
    gather x0 -> x1, local copies, waits for them, and re-layouts: none -> 3.75 us  [enter_targets(): arr_out = arr_out[(jnp.arange(k_all) - low) % k_all]]
  transfers between devices with their start and end apart: 12 -> 18, of which waited for: 5 -> 8; matrix products, arithmetic and copies ran while one was open for 12% -> 17% of each run, Pallas kernels for 0% -> 0%
where the time goes in v1:
time: 152 us; the launch traced here: 149 us
  starting transfers between devices  53.4 us (35%)
  waiting for transfers between devices  29.8 us (20%)
  local copies, waits for them, and re-layouts  28.5 us (19%)
  matrix products  27.1 us (18%)
  other arithmetic  9.51 us (6%)
    ppermute x11, starting transfers between devices, from_behind(): lax.ppermute(value, axis, [(source, source + steps) for source in range(i...  41.6 us
    ppermute x4, waiting for transfers between devices, enter_targets(): lax.ppermute(s_next[-1] if s_next else z_in, axis_name=bus_axis, perm=buf...  25.8 us
    dot_general x36, matrix products, mm(): jnp.einsum(spec, a, b, precision=highest, preferred_element_type=jnp.floa...  22.8 us
    unnamed x69, local copies, waits for them, and re-layouts  11.3 us
    ppermute x3, starting transfers between devices, enter_targets(): lax.ppermute(block_out[-1] if block_out else z_in, axis_name=bus_axis, pe...  9.78 us
    ppermute x11, waiting for transfers between devices, from_behind(): lax.ppermute(value, axis, [(source, source + steps) for source in range(i...  3.95 us
    transpose x1, local copies, waits for them, and re-layouts, set_domain_now(): panel = jnp.moveaxis(panel, 0, array_dim)  3.92 us
    gather x1, local copies, waits for them, and re-layouts, enter_targets(): arr_out = arr_out[(jnp.arange(k_all) - low) % k_all]  3.75 us
  transfers between devices with their start and end apart: 18, of which 8 were waited for; matrix products, arithmetic and copies ran while one was open for 17% of the time, Pallas kernels for 0%

profile of v1, /device:TPU:2, one launch (start us, length us, event | category | flops | bytes accessed | tf_op | source)
XLA Modules:
  0.0 149.3 jit_solution(15886612648421905361)
XLA Ops:
  4.0 3.4 %collective-permute-start = (bf16[3,3,2,128]{3,1,2,0:T(4,128)(2,1)}, bf16[3,3,2,128]{3,1,2,0:T(4,128)(2,1)}, u32[]{:S(2)}, u32[]{:S(2)}) collective-permute-start(bf16[3,3,2,128]{3,1,2,0:T(4,128)(2,1)} %pad_maximum_fusion.3), channel_id=1, source_target_pairs={{0,8},{8,16},{16,24},{24,32},{32,40},{40,48},{48,56},{56,64},{64,7... | collective-permute-start | bytes 13832 | tf_op jit(solution)/shard_map/ppermute | solution.py:52
  8.1 1.5 %slice_bitcast_fusion.33 = (f32[2,128]{1,0:T(2,128)}, f32[2,128]{1,0:T(2,128)}, f32[2,128]{1,0:T(2,128)}, f32[2,128]{1,0:T(2,128)}, f32[2,128]{1,0:T(2,128)}, /*...) fusion(f32[3,4,2,128]{3,2,1,0:T(2,128)} %param.33), kind=kLoop, calls=%fused_computation.298 | loop fusion | bytes 24576 | tf_op jit(solution)/shard_map/mul | solution.py:63
  11.7 1.2 subtract_convert_fusion
  21.4 2.6 %multiply_reduce_fusion.1 = (f32[512,2]{0,1:T(2,128)S(1)}, f32[512,2,128]{2,0,1:T(8,128)S(1)}, bf16[512,2,128]{2,0,1:T(8,128)(2,1)S(1)}) fusion(bf16[512,2,128]{2,0,1:T(8,128)(2,1)} %copy-done.4, f32[2,128]{1,0:T(2,128)} %get-tuple-element.109, bf16[3,2,128]{2,0,1:T(4,128)(2,1)S(1)} %get-tuple-element.123, f32[2,128]{1,0:T(2,128)} %get-tuple-element.110, ...), kind=kLoop, calls=%fused_computation.61 | loop fusion | flops 6683648 | bytes 1326080 | tf_op jit(solution)/shard_map/reduce_sum | solution.py:56
  25.3 1.8 %convolution_subtract_fusion.6 = f32[8,2,64,64]{3,2,1,0:T(8,128)S(1)} fusion(f32[8,2,64,64]{3,2,1,0:T(8,128)} %copy-done.1, f32[8,2,64,64]{3,2,1,0:T(8,128)S(1)} %fusion.26), kind=kOutput, calls=%fused_computation.9 | convolution fusion | flops 50397184 | bytes 786432 | tf_op jit(solution)/shard_map/...ij,...jk->...ik/dot_general | solution.py:46
  35.3 2.2 %fusion.15 = f32[8,2,128,128]{3,2,1,0:T(8,128)S(1)} fusion(f32[8,2,64,256]{3,2,1,0:T(8,128)S(1)} %fusion.5, f32[8,2,64]{2,1,0:T(2,128)S(1)} %copy.128, bf16[8,64,2,128]{3,1,0,2:T(8,128)(2,1)S(1)} %bitcast.238), kind=kOutput, calls=%fused_computation.44 | convolution fusion | flops 201588736 | bytes 1843200 | tf_op jit(solution)/shard_map/nhce,nhcf->nhef/dot_general | solution.py:46
  37.5 2.0 %fusion = f32[8,2,128,128]{3,2,1,0:T(8,128)S(1)} fusion(f32[128,128]{1,0:T(8,128)S(1)} %copy-done.6, f32[8,2]{1,0:T(8,128)S(1)} %bitcast.246, f32[8]{0:T(128)S(1)} %copy-done.24, f32[8,2,64,256]{3,2,1,0:T(8,128)S(1)} %fusion.5, f32[8,2,64]{2,1,0:T(2,128)S(1)} %copy.128, bf16[8,64,2,128]{3,1,0,2:T(8,128)(2,1)S(1)} %bitcast.239), kind=kOutput, calls=%fused_computation.2 | convolution fusion | flops 202375168 | bytes 1913344 | tf_op jit(solution)/shard_map/nhce,nhcf->nhef/dot_general | solution.py:46
  42.7 3.1 %collective-permute-start.2 = (f32[2,128,128]{2,1,0:T(8,128)S(1)}, f32[2,128,128]{2,1,0:T(8,128)S(1)}, u32[]{:S(2)}, u32[]{:S(2)}) collective-permute-start(f32[2,128,128]{2,1,0:T(8,128)S(1)} %get-tuple-element.105), channel_id=1, source_target_pairs={{0,8},{8,16},{16,24},{24,32},{32,40},{40,48},{48,56},{56,64},{64,7... | collective-permute-start | bytes 393224 | tf_op jit(solution)/shard_map/ppermute | solution.py:52
  45.9 3.4 %collective-permute-start.1 = (f32[2,128,128]{2,1,0:T(8,128)S(1)}, f32[2,128,128]{2,1,0:T(8,128)S(1)}, u32[]{:S(2)}, u32[]{:S(2)}) collective-permute-start(f32[2,128,128]{2,1,0:T(8,128)S(1)} %get-tuple-element.106), channel_id=1, source_target_pairs={{0,8},{8,16},{16,24},{24,32},{32,40},{40,48},{48,56},{56,64},{64,7... | collective-permute-start | bytes 393224 | tf_op jit(solution)/shard_map/ppermute | solution.py:52
  51.2 1.3 fusion.142
  53.0 4.3 %collective-permute-start.3 = (f32[2,128,128]{2,1,0:T(8,128)S(1)}, f32[2,128,128]{2,1,0:T(8,128)S(1)}, u32[]{:S(2)}, u32[]{:S(2)}) collective-permute-start(f32[2,128,128]{2,1,0:T(8,128)S(1)} %convolution_add_fusion.5), channel_id=1, source_target_pairs={{0,16},{8,24},{16,32},{24,40},{32,48},{40,56},{48,64},{56,72},{64,... | collective-permute-start | bytes 393224 | tf_op jit(solution)/shard_map/ppermute | solution.py:52
  57.6 4.0 %collective-permute-start.4 = (f32[2,128,128]{2,1,0:T(8,128)S(1)}, f32[2,128,128]{2,1,0:T(8,128)S(1)}, u32[]{:S(2)}, u32[]{:S(2)}) collective-permute-start(f32[2,128,128]{2,1,0:T(8,128)S(1)} %convolution_select_fusion.3), channel_id=1, source_target_pairs={{0,16},{8,24},{16,32},{24,40},{32,48},{40,56},{48,64},{56,72},{64,... | collective-permute-start | bytes 393224 | tf_op jit(solution)/shard_map/ppermute | solution.py:52
  61.9 4.1 %collective-permute-start.5 = (f32[2,128,128]{2,1,0:T(8,128)S(1)}, f32[2,128,128]{2,1,0:T(8,128)S(1)}, u32[]{:S(2)}, u32[]{:S(2)}) collective-permute-start(f32[2,128,128]{2,1,0:T(8,128)S(1)} %convolution_add_fusion.4), channel_id=1, source_target_pairs={{0,32},{8,40},{16,48},{24,56},{32,64},{40,72},{48,80},{56,88},{64,... | collective-permute-start | bytes 393224 | tf_op jit(solution)/shard_map/ppermute | solution.py:52
  66.3 4.4 %collective-permute-start.6 = (f32[2,128,128]{2,1,0:T(8,128)S(1)}, f32[2,128,128]{2,1,0:T(8,128)S(1)}, u32[]{:S(2)}, u32[]{:S(2)}) collective-permute-start(f32[2,128,128]{2,1,0:T(8,128)S(1)} %convolution_select_fusion.2), channel_id=1, source_target_pairs={{0,32},{8,40},{16,48},{24,56},{32,64},{40,72},{48,80},{56,88},{64,... | collective-permute-start | bytes 393224 | tf_op jit(solution)/shard_map/ppermute | solution.py:52
  71.1 4.5 %collective-permute-start.7 = (f32[2,128,128]{2,1,0:T(8,128)S(1)}, f32[2,128,128]{2,1,0:T(8,128)S(1)}, u32[]{:S(2)}, u32[]{:S(2)}) collective-permute-start(f32[2,128,128]{2,1,0:T(8,128)S(1)} %convolution_add_fusion.3), channel_id=1, source_target_pairs={{0,64},{8,72},{16,80},{24,88},{32,96},{40,104},{48,112},{56,120},{... | collective-permute-start | bytes 393224 | tf_op jit(solution)/shard_map/ppermute | solution.py:52
  75.8 3.4 %collective-permute-start.8 = (f32[2,128,128]{2,1,0:T(8,128)S(1)}, f32[2,128,128]{2,1,0:T(8,128)S(1)}, u32[]{:S(2)}, u32[]{:S(2)}) collective-permute-start(f32[2,128,128]{2,1,0:T(8,128)S(1)} %convolution_select_fusion.1), channel_id=1, source_target_pairs={{0,64},{8,72},{16,80},{24,88},{32,96},{40,104},{48,112},{56,120},{... | collective-permute-start | bytes 393224 | tf_op jit(solution)/shard_map/ppermute | solution.py:52
  79.5 1.8 %collective-permute-start.9 = (f32[2,128,128]{2,1,0:T(8,128)S(1)}, f32[2,128,128]{2,1,0:T(8,128)S(1)}, u32[]{:S(2)}, u32[]{:S(2)}) collective-permute-start(f32[2,128,128]{2,1,0:T(8,128)S(1)} %convolution_add_fusion.2), channel_id=1, source_target_pairs={{0,128},{8,136},{16,144},{24,152},{32,160},{40,168},{48,176},{56,1... | collective-permute-start | bytes 393224 | tf_op jit(solution)/shard_map/ppermute | solution.py:52
  82.6 5.1 %collective-permute-start.10 = (f32[2,128,128]{2,1,0:T(8,128)S(1)}, f32[2,128,128]{2,1,0:T(8,128)S(1)}, u32[]{:S(2)}, u32[]{:S(2)}) collective-permute-start(f32[2,128,128]{2,1,0:T(8,128)S(1)} %convolution_add_fusion.1), channel_id=1, source_target_pairs={{0,8},{8,16},{16,24},{24,32},{32,40},{40,48},{48,56},{56,64},{64,7... | collective-permute-start | bytes 393224 | tf_op jit(solution)/shard_map/ppermute | solution.py:52
  88.4 3.0 %collective-permute-done.10 = f32[2,128,128]{2,1,0:T(8,128)S(1)} collective-permute-done((f32[2,128,128]{2,1,0:T(8,128)S(1)}, f32[2,128,128]{2,1,0:T(8,128)S(1)}, u32[]{:S(2)}, u32[]{:S(2)}) %collective-permute-start.10) | collective-permute-done | bytes 131104 | tf_op jit(solution)/shard_map/ppermute | solution.py:52
  92.6 2.0 %collective-permute-start.11 = (bf16[512,2,128]{2,0,1:T(8,128)(2,1)S(1)}, bf16[512,2,128]{2,0,1:T(8,128)(2,1)S(1)}, u32[]{:S(2)}, u32[]{:S(2)}) collective-permute-start(bf16[512,2,128]{2,0,1:T(8,128)(2,1)S(1)} %fusion.28), channel_id=1, source_target_pairs={{0,1},{1,2},{2,3},{3,4},{4,5},{5,6},{6,7},{7,0},{8,9},{9,10},{10,1... | collective-permute-start | bytes 786440 | tf_op jit(solution)/shard_map/ppermute | solution.py:28
  94.6 10.5 %collective-permute-done.11 = bf16[512,2,128]{2,0,1:T(8,128)(2,1)S(1)} collective-permute-done((bf16[512,2,128]{2,0,1:T(8,128)(2,1)S(1)}, bf16[512,2,128]{2,0,1:T(8,128)(2,1)S(1)}, u32[]{:S(2)}, u32[]{:S(2)}) %collective-permute-start.11) | collective-permute-done | bytes 262176 | tf_op jit(solution)/shard_map/ppermute | solution.py:28
  105.1 3.2 %collective-permute-start.15 = (bf16[512,2,128]{2,0,1:T(8,128)(2,1)S(1)}, bf16[512,2,128]{2,0,1:T(8,128)(2,1)S(1)}, u32[]{:S(2)}, u32[]{:S(2)}) collective-permute-start(bf16[512,2,128]{2,0,1:T(8,128)(2,1)S(1)} %fusion.28), channel_id=1, source_target_pairs={{1,0},{2,1},{3,2},{4,3},{5,4},{6,5},{7,6},{0,7},{9,8},{10,9},{11,1... | collective-permute-start | bytes 786440 | tf_op jit(solution)/shard_map/ppermute | solution.py:32
  108.3 5.8 %collective-permute-done.12 = bf16[512,2,128]{2,0,1:T(8,128)(2,1)S(1)} collective-permute-done((bf16[512,2,128]{2,0,1:T(8,128)(2,1)S(1)}, bf16[512,2,128]{2,0,1:T(8,128)(2,1)S(1)}, u32[]{:S(2)}, u32[]{:S(2)}) %collective-permute-start.12) | collective-permute-done | bytes 262176 | tf_op jit(solution)/shard_map/ppermute | solution.py:28
  114.1 3.2 %collective-permute-start.16 = (bf16[512,2,128]{2,0,1:T(8,128)(2,1)S(1)}, bf16[512,2,128]{2,0,1:T(8,128)(2,1)S(1)}, u32[]{:S(2)}, u32[]{:S(2)}) collective-permute-start(bf16[512,2,128]{2,0,1:T(8,128)(2,1)S(1)} %collective-permute-done.15), channel_id=1, source_target_pairs={{1,0},{2,1},{3,2},{4,3},{5,4},{6,5},{7,6},{0,7},{9,8},{10,9},{11,1... | collective-permute-start | bytes 786440 | tf_op jit(solution)/shard_map/ppermute | solution.py:32
  117.3 5.0 %collective-permute-done.13 = bf16[512,2,128]{2,0,1:T(8,128)(2,1)} collective-permute-done((bf16[512,2,128]{2,0,1:T(8,128)(2,1)S(1)}, bf16[512,2,128]{2,0,1:T(8,128)(2,1)}, u32[]{:S(2)}, u32[]{:S(2)}) %collective-permute-start.13) | collective-permute-done | bytes 262176 | tf_op jit(solution)/shard_map/ppermute | solution.py:28
  122.4 3.3 %collective-permute-start.17 = (bf16[512,2,128]{2,0,1:T(8,128)(2,1)S(1)}, bf16[512,2,128]{2,0,1:T(8,128)(2,1)S(1)}, u32[]{:S(2)}, u32[]{:S(2)}) collective-permute-start(bf16[512,2,128]{2,0,1:T(8,128)(2,1)S(1)} %collective-permute-done.16), channel_id=1, source_target_pairs={{1,0},{2,1},{3,2},{4,3},{5,4},{6,5},{7,6},{0,7},{9,8},{10,9},{11,1... | collective-permute-start | bytes 786440 | tf_op jit(solution)/shard_map/ppermute | solution.py:32
  125.7 4.5 %collective-permute-done.14 = bf16[512,2,128]{2,0,1:T(8,128)(2,1)} collective-permute-done((bf16[512,2,128]{2,0,1:T(8,128)(2,1)}, bf16[512,2,128]{2,0,1:T(8,128)(2,1)}, u32[]{:S(2)}, u32[]{:S(2)}) %collective-permute-start.14) | collective-permute-done | bytes 262176 | tf_op jit(solution)/shard_map/ppermute | solution.py:28
  130.2 1.7 %bitcast_dynamic-update-slice_fusion.7 = bf16[8,512,2,128]{3,1,2,0:T(8,128)(2,1)} fusion(bf16[512,2,128]{2,0,1:T(8,128)(2,1)} %collective-permute-done.14), kind=kLoop, calls=%fused_computation.98 | loop fusion | bytes 524288
  131.9 1.7 %bitcast_dynamic-update-slice_fusion.6 = bf16[8,512,2,128]{3,1,2,0:T(8,128)(2,1)} fusion(bf16[8,512,2,128]{3,1,2,0:T(8,128)(2,1)} %bitcast_dynamic-update-slice_fusion.7, bf16[512,2,128]{2,0,1:T(8,128)(2,1)} %collective-permute-done.13), kind=kLoop, calls=%fused_computation.97 | loop fusion | bytes 524288
  138.0 3.7 %gather_fusion = bf16[8,512,2,128]{3,1,2,0:T(8,128)(2,1)} fusion(bf16[8,512,2,128]{3,1,2,0:T(8,128)(2,1)} %bitcast_dynamic-update-slice_fusion, s32[1024]{0:T(1024)S(1)} %pad_clamp_fusion), kind=kCustom, calls=%fused_computation | custom fusion | bytes 4194336 | tf_op jit(solution)/shard_map/gather | solution.py:38
  141.7 3.9 %copy.132 = bf16[512,8,2,128]{0,3,2,1:T(8,128)(2,1)} copy(bf16[512,8,2,128]{3,0,2,1:T(8,128)(2,1)} %bitcast.234) | data formatting | bytes 4194304 | tf_op jit(solution)/shard_map/transpose | solution.py:14
  145.6 3.7 %convolution_convert_fusion = bf16[512,512]{1,0:T(8,128)(2,1)} fusion(bf16[512,2048]{0,1:T(8,128)(2,1)} %bitcast.235, bf16[2048,512]{1,0:T(8,128)(2,1)S(1)} %copy-done), kind=kOutput, calls=%fused_computation.3 | convolution fusion | flops 1074003968 | bytes 4718592 | tf_op jit(solution)/shard_map/dot_general | solution.py:199
  (172 shorter events, 38.7 us)
Async XLA Ops:
  0.0 145.6 %copy-start = (bf16[2048,512]{1,0:T(8,128)(2,1)S(1)}, bf16[2048,512]{1,0:T(8,128)(2,1)}, u32[]{:S(2)}) copy-start(bf16[2048,512]{1,0:T(8,128)(2,1)} %param.35) | copy-start | bytes 6291460
  1.1 20.2 %copy-start.3 = (bf16[512,2,128]{2,0,1:T(8,128)(2,1)}, bf16[512,2,128]{2,0,1:T(8,128)(2,1)S(1)}, u32[]{:S(2)}) copy-start(bf16[512,2,128]{2,0,1:T(8,128)(2,1)S(1)} %copy.109) | copy-start | bytes 786436
  2.2 19.1 %copy-start.4 = (bf16[512,2,128]{2,0,1:T(8,128)(2,1)}, bf16[512,2,128]{2,0,1:T(8,128)(2,1)S(1)}, u32[]{:S(2)}) copy-start(bf16[512,2,128]{2,0,1:T(8,128)(2,1)S(1)} %copy.108) | copy-start | bytes 786436
  4.0 16.7 %collective-permute-start = (bf16[3,3,2,128]{3,1,2,0:T(4,128)(2,1)}, bf16[3,3,2,128]{3,1,2,0:T(4,128)(2,1)}, u32[]{:S(2)}, u32[]{:S(2)}) collective-permute-start(bf16[3,3,2,128]{3,1,2,0:T(4,128)(2,1)} %pad_maximum_fusion.3), channel_id=1, source_target_pairs={{0,8},{8,16},{16,24},{24,32},{32,40},{40,48},{48,56},{56,64},{64,7... | collective-permute-start | bytes 13832 | tf_op jit(solution)/shard_map/ppermute | solution.py:52
  8.1 9.0 %copy-start.5 = (f32[128,128]{1,0:T(8,128)}, f32[128,128]{1,0:T(8,128)S(1)}, u32[]{:S(2)}) copy-start(f32[128,128]{1,0:T(8,128)S(1)} %fusion.84) | copy-start | bytes 196612
  18.5 6.1 %copy-start.1 = (f32[8,2,64,64]{3,2,1,0:T(8,128)}, f32[8,2,64,64]{3,2,1,0:T(8,128)S(1)}, u32[]{:S(2)}) copy-start(f32[8,2,64,64]{3,2,1,0:T(8,128)S(1)} %broadcast_in_dim.63) | copy-start | bytes 786436
  20.6 3.6 %copy-start.18 = (f32[8,2,64]{2,1,0:T(2,128)S(1)}, f32[8,2,64]{2,1,0:T(2,128)}, u32[]{:S(2)}) copy-start(f32[8,2,64]{2,1,0:T(2,128)} %copy.105) | copy-start | bytes 12292
  20.6 4.0 %copy-start.12 = (pred[64,64]{1,0:T(8,128)(4,1)S(1)}, pred[64,64]{1,0:T(8,128)(4,1)}, u32[]{:S(2)}) copy-start(pred[64,64]{1,0:T(8,128)(4,1)} %get-tuple-element.130) | copy-start | bytes 12292
  41.1 8.2 %copy-start.2 = (f32[8,2,128,256]{3,2,1,0:T(8,128)S(1)}, f32[8,2,128,256]{3,2,1,0:T(8,128)}, u32[]{:S(2)}) copy-start(f32[8,2,128,256]{3,2,1,0:T(8,128)} %fusion.41) | copy-start | bytes 6291460
  42.7 6.8 %copy-start.20 = (f32[2,128]{1,0:T(2,128)S(1)}, f32[2,128]{1,0:T(2,128)}, u32[]{:S(2)}) copy-start(f32[2,128]{1,0:T(2,128)} %get-tuple-element.113) | copy-start | bytes 3076
  42.7 6.8 %copy-start.21 = (f32[2,128]{1,0:T(2,128)S(1)}, f32[2,128]{1,0:T(2,128)}, u32[]{:S(2)}) copy-start(f32[2,128]{1,0:T(2,128)} %get-tuple-element.114) | copy-start | bytes 3076
  42.7 6.8 %copy-start.22 = (f32[2,128]{1,0:T(2,128)S(1)}, f32[2,128]{1,0:T(2,128)}, u32[]{:S(2)}) copy-start(f32[2,128]{1,0:T(2,128)} %get-tuple-element.115) | copy-start | bytes 3076
  42.7 6.8 %copy-start.23 = (f32[2,128]{1,0:T(2,128)S(1)}, f32[2,128]{1,0:T(2,128)}, u32[]{:S(2)}) copy-start(f32[2,128]{1,0:T(2,128)} %get-tuple-element.116) | copy-start | bytes 3076
  42.7 14.6 %collective-permute-start.2 = (f32[2,128,128]{2,1,0:T(8,128)S(1)}, f32[2,128,128]{2,1,0:T(8,128)S(1)}, u32[]{:S(2)}, u32[]{:S(2)}) collective-permute-start(f32[2,128,128]{2,1,0:T(8,128)S(1)} %get-tuple-element.105), channel_id=1, source_target_pairs={{0,8},{8,16},{16,24},{24,32},{32,40},{40,48},{48,56},{56,64},{64,7... | collective-permute-start | bytes 393224 | tf_op jit(solution)/shard_map/ppermute | solution.py:52
  45.9 6.9 %collective-permute-start.1 = (f32[2,128,128]{2,1,0:T(8,128)S(1)}, f32[2,128,128]{2,1,0:T(8,128)S(1)}, u32[]{:S(2)}, u32[]{:S(2)}) collective-permute-start(f32[2,128,128]{2,1,0:T(8,128)S(1)} %get-tuple-element.106), channel_id=1, source_target_pairs={{0,8},{8,16},{16,24},{24,32},{32,40},{40,48},{48,56},{56,64},{64,7... | collective-permute-start | bytes 393224 | tf_op jit(solution)/shard_map/ppermute | solution.py:52
  53.0 8.7 %collective-permute-start.3 = (f32[2,128,128]{2,1,0:T(8,128)S(1)}, f32[2,128,128]{2,1,0:T(8,128)S(1)}, u32[]{:S(2)}, u32[]{:S(2)}) collective-permute-start(f32[2,128,128]{2,1,0:T(8,128)S(1)} %convolution_add_fusion.5), channel_id=1, source_target_pairs={{0,16},{8,24},{16,32},{24,40},{32,48},{40,56},{48,64},{56,72},{64,... | collective-permute-start | bytes 393224 | tf_op jit(solution)/shard_map/ppermute | solution.py:52
  57.6 8.4 %collective-permute-start.4 = (f32[2,128,128]{2,1,0:T(8,128)S(1)}, f32[2,128,128]{2,1,0:T(8,128)S(1)}, u32[]{:S(2)}, u32[]{:S(2)}) collective-permute-start(f32[2,128,128]{2,1,0:T(8,128)S(1)} %convolution_select_fusion.3), channel_id=1, source_target_pairs={{0,16},{8,24},{16,32},{24,40},{32,48},{40,56},{48,64},{56,72},{64,... | collective-permute-start | bytes 393224 | tf_op jit(solution)/shard_map/ppermute | solution.py:52
  61.9 8.8 %collective-permute-start.5 = (f32[2,128,128]{2,1,0:T(8,128)S(1)}, f32[2,128,128]{2,1,0:T(8,128)S(1)}, u32[]{:S(2)}, u32[]{:S(2)}) collective-permute-start(f32[2,128,128]{2,1,0:T(8,128)S(1)} %convolution_add_fusion.4), channel_id=1, source_target_pairs={{0,32},{8,40},{16,48},{24,56},{32,64},{40,72},{48,80},{56,88},{64,... | collective-permute-start | bytes 393224 | tf_op jit(solution)/shard_map/ppermute | solution.py:52
  66.3 9.2 %collective-permute-start.6 = (f32[2,128,128]{2,1,0:T(8,128)S(1)}, f32[2,128,128]{2,1,0:T(8,128)S(1)}, u32[]{:S(2)}, u32[]{:S(2)}) collective-permute-start(f32[2,128,128]{2,1,0:T(8,128)S(1)} %convolution_select_fusion.2), channel_id=1, source_target_pairs={{0,32},{8,40},{16,48},{24,56},{32,64},{40,72},{48,80},{56,88},{64,... | collective-permute-start | bytes 393224 | tf_op jit(solution)/shard_map/ppermute | solution.py:52
  71.1 8.2 %collective-permute-start.7 = (f32[2,128,128]{2,1,0:T(8,128)S(1)}, f32[2,128,128]{2,1,0:T(8,128)S(1)}, u32[]{:S(2)}, u32[]{:S(2)}) collective-permute-start(f32[2,128,128]{2,1,0:T(8,128)S(1)} %convolution_add_fusion.3), channel_id=1, source_target_pairs={{0,64},{8,72},{16,80},{24,88},{32,96},{40,104},{48,112},{56,120},{... | collective-permute-start | bytes 393224 | tf_op jit(solution)/shard_map/ppermute | solution.py:52
  75.8 5.9 %collective-permute-start.8 = (f32[2,128,128]{2,1,0:T(8,128)S(1)}, f32[2,128,128]{2,1,0:T(8,128)S(1)}, u32[]{:S(2)}, u32[]{:S(2)}) collective-permute-start(f32[2,128,128]{2,1,0:T(8,128)S(1)} %convolution_select_fusion.1), channel_id=1, source_target_pairs={{0,64},{8,72},{16,80},{24,88},{32,96},{40,104},{48,112},{56,120},{... | collective-permute-start | bytes 393224 | tf_op jit(solution)/shard_map/ppermute | solution.py:52
  79.5 2.8 %collective-permute-start.9 = (f32[2,128,128]{2,1,0:T(8,128)S(1)}, f32[2,128,128]{2,1,0:T(8,128)S(1)}, u32[]{:S(2)}, u32[]{:S(2)}) collective-permute-start(f32[2,128,128]{2,1,0:T(8,128)S(1)} %convolution_add_fusion.2), channel_id=1, source_target_pairs={{0,128},{8,136},{16,144},{24,152},{32,160},{40,168},{48,176},{56,1... | collective-permute-start | bytes 393224 | tf_op jit(solution)/shard_map/ppermute | solution.py:52
  82.6 9.8 %copy-start.7 = (bf16[512,2,128]{2,1,0:T(2,128)(2,1)S(1)}, bf16[512,2,128]{2,1,0:T(2,128)(2,1)}, u32[]{:S(2)}) copy-start(bf16[512,2,128]{2,1,0:T(2,128)(2,1)} %param.29) | copy-start | bytes 786436
  82.6 9.7 %copy-start.25 = (f32[128]{0:T(128)S(1)}, f32[128]{0:T(128)}, u32[]{:S(2)}) copy-start(f32[128]{0:T(128)} %param.34) | copy-start | bytes 1540
  82.6 8.8 %collective-permute-start.10 = (f32[2,128,128]{2,1,0:T(8,128)S(1)}, f32[2,128,128]{2,1,0:T(8,128)S(1)}, u32[]{:S(2)}, u32[]{:S(2)}) collective-permute-start(f32[2,128,128]{2,1,0:T(8,128)S(1)} %convolution_add_fusion.1), channel_id=1, source_target_pairs={{0,8},{8,16},{16,24},{24,32},{32,40},{40,48},{48,56},{56,64},{64,7... | collective-permute-start | bytes 393224 | tf_op jit(solution)/shard_map/ppermute | solution.py:52
  92.6 12.5 %collective-permute-start.11 = (bf16[512,2,128]{2,0,1:T(8,128)(2,1)S(1)}, bf16[512,2,128]{2,0,1:T(8,128)(2,1)S(1)}, u32[]{:S(2)}, u32[]{:S(2)}) collective-permute-start(bf16[512,2,128]{2,0,1:T(8,128)(2,1)S(1)} %fusion.28), channel_id=1, source_target_pairs={{0,1},{1,2},{2,3},{3,4},{4,5},{5,6},{6,7},{7,0},{8,9},{9,10},{10,1... | collective-permute-start | bytes 786440 | tf_op jit(solution)/shard_map/ppermute | solution.py:28
  105.1 9.0 %collective-permute-start.12 = (bf16[512,2,128]{2,0,1:T(8,128)(2,1)S(1)}, bf16[512,2,128]{2,0,1:T(8,128)(2,1)S(1)}, u32[]{:S(2)}, u32[]{:S(2)}) collective-permute-start(bf16[512,2,128]{2,0,1:T(8,128)(2,1)S(1)} %collective-permute-done.11), channel_id=1, source_target_pairs={{0,1},{1,2},{2,3},{3,4},{4,5},{5,6},{6,7},{7,0},{8,9},{9,10},{10,1... | collective-permute-start | bytes 786440 | tf_op jit(solution)/shard_map/ppermute | solution.py:28
  105.1 9.0 %collective-permute-start.15 = (bf16[512,2,128]{2,0,1:T(8,128)(2,1)S(1)}, bf16[512,2,128]{2,0,1:T(8,128)(2,1)S(1)}, u32[]{:S(2)}, u32[]{:S(2)}) collective-permute-start(bf16[512,2,128]{2,0,1:T(8,128)(2,1)S(1)} %fusion.28), channel_id=1, source_target_pairs={{1,0},{2,1},{3,2},{4,3},{5,4},{6,5},{7,6},{0,7},{9,8},{10,9},{11,1... | collective-permute-start | bytes 786440 | tf_op jit(solution)/shard_map/ppermute | solution.py:32
  114.1 8.2 %collective-permute-start.13 = (bf16[512,2,128]{2,0,1:T(8,128)(2,1)S(1)}, bf16[512,2,128]{2,0,1:T(8,128)(2,1)}, u32[]{:S(2)}, u32[]{:S(2)}) collective-permute-start(bf16[512,2,128]{2,0,1:T(8,128)(2,1)S(1)} %collective-permute-done.12), channel_id=1, source_target_pairs={{0,1},{1,2},{2,3},{3,4},{4,5},{5,6},{6,7},{7,0},{8,9},{9,10},{10,1... | collective-permute-start | bytes 786440 | tf_op jit(solution)/shard_map/ppermute | solution.py:28
  114.1 8.3 %collective-permute-start.16 = (bf16[512,2,128]{2,0,1:T(8,128)(2,1)S(1)}, bf16[512,2,128]{2,0,1:T(8,128)(2,1)S(1)}, u32[]{:S(2)}, u32[]{:S(2)}) collective-permute-start(bf16[512,2,128]{2,0,1:T(8,128)(2,1)S(1)} %collective-permute-done.15), channel_id=1, source_target_pairs={{1,0},{2,1},{3,2},{4,3},{5,4},{6,5},{7,6},{0,7},{9,8},{10,9},{11,1... | collective-permute-start | bytes 786440 | tf_op jit(solution)/shard_map/ppermute | solution.py:32
  122.3 7.9 %collective-permute-start.14 = (bf16[512,2,128]{2,0,1:T(8,128)(2,1)}, bf16[512,2,128]{2,0,1:T(8,128)(2,1)}, u32[]{:S(2)}, u32[]{:S(2)}) collective-permute-start(bf16[512,2,128]{2,0,1:T(8,128)(2,1)} %collective-permute-done.13), channel_id=1, source_target_pairs={{0,1},{1,2},{2,3},{3,4},{4,5},{5,6},{6,7},{7,0},{8,9},{9,10},{10,1... | collective-permute-start | bytes 786440 | tf_op jit(solution)/shard_map/ppermute | solution.py:28
  122.4 14.9 %collective-permute-start.17 = (bf16[512,2,128]{2,0,1:T(8,128)(2,1)S(1)}, bf16[512,2,128]{2,0,1:T(8,128)(2,1)S(1)}, u32[]{:S(2)}, u32[]{:S(2)}) collective-permute-start(bf16[512,2,128]{2,0,1:T(8,128)(2,1)S(1)} %collective-permute-done.16), channel_id=1, source_target_pairs={{1,0},{2,1},{3,2},{4,3},{5,4},{6,5},{7,6},{0,7},{9,8},{10,9},{11,1... | collective-permute-start | bytes 786440 | tf_op jit(solution)/shard_map/ppermute | solution.py:32
  (12 other events, 33.6 us)
